TPU v7x, 32 devices: a whole 2x2x4 slice. The times are simulated.
32 devices in a mesh: cell: 8 (over y, x, core), gene: 4 (over z).
Axes of the slice: x: 2, y: 2, z: 4, core: 2. Of those that a mesh axis runs over, the one named last changes fastest.
Arguments:
- counts: int32 [2048, 2560], P('cell', 'gene'), may hold values from 1 to 8
- cell_factors: float32 [64, 2048], P(None, 'cell'), may hold values from -6 to 6
- loadings: float32 [64, 2560], P(None, 'gene'), may hold values from -3 to 3
- cell_momenta: float32 [64, 2048], P(None, 'cell'), may hold values from -6 to 6
- loading_momenta: float32 [64, 2560], P(None, 'gene'), may hold values from -6 to 6
- step: float32 [64], replicated, may hold values from 0.01 to 0.04
Outputs:
- new_factors: float32 [64, 2048], P(None, 'cell')
- new_loadings: float32 [64, 2560], P(None, 'gene')
- new_cell_momenta: float32 [64, 2048], P(None, 'cell')
- new_loading_momenta: float32 [64, 2560], P(None, 'gene')
- log_rate: bfloat16 [2048, 2560], P('cell', 'gene')
All inputs are finite; a program needn't handle non-finite values.
Results may differ from a plain program's by a relative error of at most 0.001.
Values sent between devices are 32-bit elements; how exact they have to be, the bound alone decides.
No kernel may reach another device: no remote copies, remote signals or barrier semaphores. Data moves between devices by JAX's collectives and lax.ppermute only.
A program may use at most 64 MiB of HBM per device.

v0:
```python
import jax
import jax.numpy as jnp
from jax import lax
from jax.sharding import PartitionSpec as P

K = 64


def local(counts, cell_factors, loadings, cell_momenta, loading_momenta, step):
    scale = 1.0 / jnp.sqrt(jnp.float32(K))
    counts_float = counts.astype(jnp.float32)
    library = lax.psum(jnp.sum(counts_float, axis=1), "gene")
    genes_total = jnp.float32(loadings.shape[1] * lax.axis_size("gene"))
    half = 0.5 * step[:, None]
    full = step[:, None]
    width = loadings.shape[1] // lax.axis_size("cell")
    offset = lax.axis_index("cell") * width

    def gradient(factors, loads, own_loads):
        linear = (
            lax.dot_general(
                factors, loads, (((0,), (0,)), ((), ())), precision=lax.Precision.HIGHEST
            )
            * scale
        )
        expo = jnp.exp(linear)
        squares = jnp.sum(loads * loads, axis=1)
        total, squares = lax.psum((jnp.sum(expo, axis=1), squares), "gene")
        size = library / total
        resid = counts_float - size[:, None] * expo
        cross = (
            lax.dot_general(loads, resid, (((1,), (1,)), ((), ())), precision=lax.Precision.HIGHEST)
            * scale
        )
        grad_u = lax.psum(cross, "gene") - factors
        ard = (genes_total + 2.0) / (squares + 2.0)
        part_v = jnp.dot(factors, resid, precision=lax.Precision.HIGHEST) * scale
        grad_v = (
            lax.psum_scatter(part_v, "cell", scatter_dimension=1, tiled=True)
            - ard[:, None] * own_loads
        )
        return (grad_u, grad_v, linear, size)

    factors = cell_factors
    mom_u = cell_momenta
    loads = loadings
    own = lax.dynamic_slice_in_dim(loadings, offset, width, 1)
    mom_v = lax.dynamic_slice_in_dim(loading_momenta, offset, width, 1)
    grad_u, grad_v, linear, size = gradient(factors, loads, own)
    mom_u = mom_u + half * grad_u
    mom_v = mom_v + half * grad_v
    factors = factors + full * mom_u
    own = own + full * mom_v
    loads = lax.all_gather(own, "cell", axis=1, tiled=True)
    grad_u, grad_v, linear, size = gradient(factors, loads, own)
    mom_u = mom_u + half * grad_u
    mom_v = mom_v + half * grad_v
    mom_v = lax.all_gather(mom_v, "cell", axis=1, tiled=True)
    rates = (linear + jnp.log(size)[:, None]).astype(jnp.bfloat16)
    return (factors, loads, mom_u, mom_v, rates)


def solution(mesh):
    placed = (
        P("cell", "gene"),
        P(None, "cell"),
        P(None, "gene"),
        P(None, "cell"),
        P(None, "gene"),
        P(),
    )
    return jax.shard_map(
        local,
        mesh=mesh,
        in_specs=placed,
        out_specs=(
            P(None, "cell"),
            P(None, "gene"),
            P(None, "cell"),
            P(None, "gene"),
            P("cell", "gene"),
        ),
        check_vma=False,
    )
```

profile of v0, /device:TPU:0, one launch (start us, length us, event | category | flops | bytes accessed | tf_op | source)
XLA Modules:
  0.0 142.7 jit_solution(1274128571875531226)
XLA Ops:
  8.1 1.1 multiply_reduce_fusion.1
  9.2 1.3 convert_reduce_fusion
  10.5 0.9 fusion.5
  11.3 13.5 %all-reduce.1 = (f32[256]{0:T(256)S(1)}, f32[256]{0:T(256)S(1)}, f32[64]{0:T(128)S(1)}) all-reduce(f32[256]{0:T(256)S(1)} %convert_reduce_fusion, f32[256]{0:T(256)S(1)} %get-tuple-element.12, f32[64]{0:T(128)S(1)} %multiply_reduce_fusion.1), channel_id=1, replica_groups=mesh['cell'=8,'gene'=4] {'gene'}, use_global_device_ids=true, to_apply=%region_1.0 | all-reduce | flops 576 | bytes 4608 | tf_op jit(solution)/shard_map/psum | solution.py:12
  24.8 1.5 %fusion.2 = f32[64,256]{1,0:T(8,128)} fusion(f32[64,640]{1,0:T(8,128)S(1)} %copy-done.2, f32[256,640]{1,0:T(8,128)S(1)} %get-tuple-element.13, s32[256,640]{1,0:T(8,128)S(1)} %copy-done, f32[256]{0:T(256)S(1)} %div.12), kind=kOutput, calls=%fused_computation.8 | convolution fusion | flops 126337024 | bytes 1541120 | tf_op jit(solution)/shard_map/dot_general | solution.py:32
  27.0 0.9 copy.15
  28.6 30.4 %all-reduce.5.cloned.1.call-done = f32[64,256]{1,0:T(8,128)} async-done(((f32[64,256]{1,0:T(8,128)}), f32[64,256]{1,0:T(8,128)}) %all-reduce.5.cloned.1.call-update) | async-done | bytes 65552 | tf_op jit(solution)/shard_map/psum | solution.py:35
  59.0 0.9 multiply_add_fusion.1
  59.9 2.5 %reduce-scatter.7.cloned.1.call-done = f32[80,64]{1,0:T(8,128)} async-done(((f32[640,64]{1,0:T(8,128)}), f32[80,64]{1,0:T(8,128)}) %reduce-scatter.7.cloned.1.call-update) | async-done | bytes 20496
  62.5 0.8 copy.16
  63.3 1.0 fusion.3
  64.3 9.3 %all-gather = f32[8,80,64]{1,2,0:T(8,128)S(1)} all-gather(f32[1,80,64]{1,2,0:T(8,128)S(1)} %fusion.3), channel_id=1, replica_groups=mesh['cell'=8,'gene'=4] {'cell'}, dimensions={0}, use_global_device_ids=true | all-gather | bytes 184320 | tf_op jit(solution)/shard_map/all_gather | solution.py:54
  74.0 0.9 exponential_reduce_fusion
  74.8 11.7 %all-reduce = (f32[256]{0:T(256)S(1)}, f32[64]{0:T(128)S(1)}) all-reduce(f32[256]{0:T(256)S(1)} %get-tuple-element.14, f32[64]{0:T(128)S(1)} %multiply_reduce_fusion), channel_id=1, replica_groups=mesh['cell'=8,'gene'=4] {'gene'}, use_global_device_ids=true, to_apply=%region_9.0 | all-reduce | flops 320 | bytes 2560 | tf_op jit(solution)/shard_map/psum | solution.py:28
  86.5 1.5 %convolution_multiply_fusion.4 = f32[64,256]{1,0:T(8,128)} fusion(f32[640,64]{0,1:T(8,128)S(1)} %reshape.19, s32[256,640]{1,0:T(8,128)S(1)} %copy-done, f32[256,640]{1,0:T(8,128)S(1)} %get-tuple-element.15, f32[256]{0:T(256)S(1)} %get-tuple-element.11), kind=kOutput, calls=%fused_computation.6 | convolution fusion | flops 126337024 | bytes 1541120 | tf_op jit(solution)/shard_map/dot_general | solution.py:32
  88.7 0.8 add_convert_fusion
  89.5 0.9 copy.17
  90.5 29.9 %all-reduce.7.cloned.1.call-done = f32[64,256]{1,0:T(8,128)} async-done(((f32[64,256]{1,0:T(8,128)}), f32[64,256]{1,0:T(8,128)}) %all-reduce.7.cloned.1.call-update) | async-done | bytes 65552 | tf_op jit(solution)/shard_map/psum | solution.py:35
  120.3 1.5 %multiply_add_fusion = f32[64,256]{1,0:T(8,128)} fusion(f32[64,256]{1,0:T(8,128)} %all-reduce.7.cloned.1.call-done, f32[64,256]{1,0:T(8,128)S(1)} %multiply_add_fusion.1, f32[64]{0:T(128)S(1)} %broadcast_multiply_fusion, f32[64,256]{1,0:T(8,128)S(1)} %copy-done.5, f32[64,256]{1,0:T(8,128)S(1)} %copy-done.6, f32[64,256]{1,0:T(8,128)S(1)} %copy-done.3), kind=kLoop, calls=%fused_computation.16 | loop fusion | flops 98304 | bytes 393472 | tf_op jit(solution)/shard_map/add | solution.py:56
  121.9 1.4 reduce-scatter.9.cloned.1.call-done
  123.2 0.8 copy.18
  124.1 1.0 add_bitcast_fusion
  125.1 9.3 %all-gather.1 = f32[8,80,64]{1,2,0:T(8,128)S(1)} all-gather(f32[1,80,64]{1,2,0:T(8,128)S(1)} %add_bitcast_fusion), channel_id=1, replica_groups=mesh['cell'=8,'gene'=4] {'cell'}, dimensions={0}, use_global_device_ids=true | all-gather | bytes 184320 | tf_op jit(solution)/shard_map/all_gather | solution.py:58
  134.5 0.8 reshape.21
  (35 shorter events, 2.7 us)
Async XLA Ops:
  8.0 51.0 %all-reduce.5.cloned.1.call-start = ((), (), s32[]{:S(2)}) async-start(), calls=%async_computation.2 | async-start | bytes 131072 | tf_op jit(solution)/shard_map/psum | solution.py:35
  8.0 2.4 %copy-start.2 = (f32[64,640]{1,0:T(8,128)S(1)}, f32[64,640]{1,0:T(8,128)}, u32[]{:S(2)}) copy-start(f32[64,640]{1,0:T(8,128)} %param.8) | copy-start | bytes 491524
  8.1 2.4 %copy-start.3 = (f32[64,256]{1,0:T(8,128)S(1)}, f32[64,256]{1,0:T(8,128)}, u32[]{:S(2)}) copy-start(f32[64,256]{1,0:T(8,128)} %param.7) | copy-start | bytes 196612
  9.1 15.7 %copy-start = (s32[256,640]{1,0:T(8,128)S(1)}, s32[256,640]{1,0:T(8,128)}, u32[]{:S(2)}) copy-start(s32[256,640]{1,0:T(8,128)} %param.6) | copy-start | bytes 1966084
  26.3 36.1 %reduce-scatter.7.cloned.1.call-start = ((), (), s32[]{:S(2)}) async-start(), calls=%async_computation.4 | async-start | bytes 368640
  27.9 0.7 copy-start.7
  27.9 31.1 %copy-start.5 = (f32[64,256]{1,0:T(8,128)S(1)}, f32[64,256]{1,0:T(8,128)}, u32[]{:S(2)}) copy-start(f32[64,256]{1,0:T(8,128)} %param.9) | copy-start | bytes 196612
  27.9 92.4 %all-reduce.7.cloned.1.call-start = ((), (), s32[]{:S(2)}) async-start(), calls=%async_computation.3 | async-start | bytes 131072 | tf_op jit(solution)/shard_map/psum | solution.py:35
  59.9 60.4 %copy-start.4 = (f32[64,256]{1,0:T(8,128)}, f32[64,256]{1,0:T(8,128)S(1)}, u32[]{:S(2)}) copy-start(f32[64,256]{1,0:T(8,128)S(1)} %multiply_add_fusion.1) | copy-start | bytes 196612
  73.8 12.7 %copy-start.1 = (f32[640,64]{0,1:T(8,128)}, f32[640,64]{0,1:T(8,128)S(1)}, u32[]{:S(2)}) copy-start(f32[640,64]{0,1:T(8,128)S(1)} %reshape.19) | copy-start | bytes 491524
  88.7 34.6 %reduce-scatter.9.cloned.1.call-start = ((), (), s32[]{:S(2)}) async-start(), calls=%async_computation.5 | async-start | bytes 368640
  90.4 29.9 %copy-start.6 = (f32[64,256]{1,0:T(8,128)S(1)}, f32[64,256]{1,0:T(8,128)}, u32[]{:S(2)}) copy-start(f32[64,256]{1,0:T(8,128)} %all-reduce.5.cloned.1.call-done) | copy-start | bytes 196612
Sparse Core Ops, SparseCore 0:
  26.5 32.5 all-reduce.4
  88.8 31.5 all-reduce.6
Sparse Core Ops, SparseCore 1:
  30.4 32.0 reduce-scatter.6
  92.2 31.0 reduce-scatter.8
where the time goes:
time: 143 us
  waiting for transfers between devices  64.2 us (45%)
  blocking collectives  43.7 us (31%)
  between operations  15.6 us (11%)
  other arithmetic  7.73 us (5%)
  matrix products  5.94 us (4%)
  local copies, waits for them, and re-layouts  5.32 us (4%)
    psum x2, waiting for transfers between devices, gradient(): grad_u = lax.psum(cross, 'gene') - factors  60.3 us
    psum x1, blocking collectives, local(): library = lax.psum(jnp.sum(counts_float, axis=1), 'gene')  13.5 us
    psum x1, blocking collectives, gradient(): total, squares = lax.psum((jnp.sum(expo, axis=1), squares), 'gene')  11.7 us
    all_gather x1, blocking collectives, local(): loads = lax.all_gather(own, 'cell', axis=1, tiled=True)  9.26 us
    all_gather x1, blocking collectives, local(): mom_v = lax.all_gather(mom_v, 'cell', axis=1, tiled=True)  9.26 us
    unnamed x22, local copies, waits for them, and re-layouts  5.01 us
    unnamed x6, waiting for transfers between devices  3.93 us
    dot_general x2, matrix products, gradient(): lax.dot_general(loads, resid, (((1,), (1,)), ((), ())), precision=lax.Pre...  2.98 us
  transfers between devices with their start and end apart: 4, of which 4 were waited for; matrix products, arithmetic and copies ran while one was open for 4% of the time, Pallas kernels for 0%

commit v1 on v0

--- a/solution.py
+++ b/solution.py
@@ -4,6 +4,11 @@
 from jax.sharding import PartitionSpec as P
 
 K = 64
+
+
+def summed_here(shard, axis):
+    blocks = lax.all_gather(shard, axis)
+    return jnp.sum(blocks, axis=0)
 
 
 def local(counts, cell_factors, loadings, cell_momenta, loading_momenta, step):
@@ -32,7 +37,7 @@
             lax.dot_general(loads, resid, (((1,), (1,)), ((), ())), precision=lax.Precision.HIGHEST)
             * scale
         )
-        grad_u = lax.psum(cross, "gene") - factors
+        grad_u = summed_here(cross, "gene") - factors
         ard = (genes_total + 2.0) / (squares + 2.0)
         part_v = jnp.dot(factors, resid, precision=lax.Precision.HIGHEST) * scale
         grad_v = (

time: 143 us -> 149 us (1.042)
  blocking collectives: 43.7 us -> 71.3 us
  waiting for transfers between devices: 64.2 us -> 46.9 us
  other arithmetic: 7.73 us -> 4.95 us
    psum x2 -> x0, waiting for transfers between devices: 60.3 us -> none  [gradient(): grad_u = lax.psum(cross, 'gene') - factors]
    unnamed x6 -> x4, waiting for transfers between devices: 3.93 us -> 46.9 us
    all_gather x0 -> x2, blocking collectives: none -> 27.6 us  [summed_here(): blocks = lax.all_gather(shard, axis)]
    unnamed x22 -> x20, local copies, waits for them, and re-layouts: 5.01 us -> 5.25 us
  transfers between devices with their start and end apart: 4 -> 2, of which waited for: 4 -> 2; matrix products, arithmetic and copies ran while one was open for 4% -> 1% of each run, Pallas kernels for 0% -> 0%
where the time goes in v1:
time: 149 us
  blocking collectives  71.3 us (48%)
  waiting for transfers between devices  46.9 us (31%)
  between operations  14.2 us (10%)
  local copies, waits for them, and re-layouts  5.57 us (4%)
  matrix products  5.51 us (4%)
  other arithmetic  4.95 us (3%)
    unnamed x4, waiting for transfers between devices  46.9 us
    all_gather x2, blocking collectives, summed_here(): blocks = lax.all_gather(shard, axis)  27.6 us
    psum x1, blocking collectives, local(): library = lax.psum(jnp.sum(counts_float, axis=1), 'gene')  13.5 us
    psum x1, blocking collectives, gradient(): total, squares = lax.psum((jnp.sum(expo, axis=1), squares), 'gene')  11.7 us
    all_gather x1, blocking collectives, local(): mom_v = lax.all_gather(mom_v, 'cell', axis=1, tiled=True)  9.28 us
    all_gather x1, blocking collectives, local(): loads = lax.all_gather(own, 'cell', axis=1, tiled=True)  9.26 us
    unnamed x20, local copies, waits for them, and re-layouts  5.25 us
  transfers between devices with their start and end apart: 2, of which 2 were waited for; matrix products, arithmetic and copies ran while one was open for 1% of the time, Pallas kernels for 0%

profile of v1, /device:TPU:0, one launch (start us, length us, event | category | flops | bytes accessed | tf_op | source)
XLA Modules:
  0.0 148.6 jit_solution(15875680369450176986)
XLA Ops:
  7.2 1.1 multiply_reduce_fusion.1
  8.3 1.7 %fusion.5 = (f32[256]{0:T(256)S(1)}, f32[256,640]{1,0:T(8,128)S(1)}) fusion(f32[64,256]{1,0:T(8,128)} %param.7, f32[64,640]{1,0:T(8,128)S(1)} %copy-done.2), kind=kOutput, calls=%fused_computation.27 | convolution fusion | flops 126156544 | bytes 885760 | tf_op jit(solution)/shard_map/dot_general | solution.py:26
  10.2 13.5 %all-reduce.1 = (f32[256]{0:T(256)S(1)}, f32[256]{0:T(256)S(1)}, f32[64]{0:T(128)S(1)}) all-reduce(f32[256]{0:T(256)S(1)} %convert_reduce_fusion, f32[256]{0:T(256)S(1)} %get-tuple-element.12, f32[64]{0:T(128)S(1)} %multiply_reduce_fusion.1), channel_id=1, replica_groups=mesh['cell'=8,'gene'=4] {'gene'}, use_global_device_ids=true, to_apply=%region_1.0 | all-reduce | flops 576 | bytes 4608 | tf_op jit(solution)/shard_map/psum | solution.py:17
  23.7 0.6 fusion.1
  24.3 0.9 copy.15
  25.3 0.9 fusion.2
  26.2 13.8 %all-gather = f32[256,256]{1,0:T(8,128)S(1)} all-gather(f32[64,256]{1,0:T(8,128)S(1)} %fusion.2), channel_id=2, replica_groups=mesh['cell'=8,'gene'=4] {'gene'}, dimensions={0}, use_global_device_ids=true | all-gather | bytes 327680 | tf_op jit(solution)/shard_map/all_gather | solution.py:10
  40.0 0.8 copy-done.5
  41.0 16.4 %reduce-scatter.7.cloned.1.call-done = f32[80,64]{1,0:T(8,128)} async-done(((f32[640,64]{1,0:T(8,128)}), f32[80,64]{1,0:T(8,128)}) %reduce-scatter.7.cloned.1.call-update) | async-done | bytes 20496
  57.4 0.8 copy.16
  58.3 1.0 fusion.3
  59.2 9.3 %all-gather.2 = f32[8,80,64]{1,2,0:T(8,128)S(1)} all-gather(f32[1,80,64]{1,2,0:T(8,128)S(1)} %fusion.3), channel_id=1, replica_groups=mesh['cell'=8,'gene'=4] {'cell'}, dimensions={0}, use_global_device_ids=true | all-gather | bytes 184320 | tf_op jit(solution)/shard_map/all_gather | solution.py:59
  68.9 0.9 exponential_reduce_fusion
  69.8 11.7 %all-reduce = (f32[256]{0:T(256)S(1)}, f32[64]{0:T(128)S(1)}) all-reduce(f32[256]{0:T(256)S(1)} %get-tuple-element.14, f32[64]{0:T(128)S(1)} %multiply_reduce_fusion), channel_id=1, replica_groups=mesh['cell'=8,'gene'=4] {'gene'}, use_global_device_ids=true, to_apply=%region_9.0 | all-reduce | flops 320 | bytes 2560 | tf_op jit(solution)/shard_map/psum | solution.py:33
  81.5 0.8 convolution_multiply_fusion.4
  82.9 13.8 %all-gather.1 = f32[256,256]{1,0:T(8,128)S(1)} all-gather(f32[64,256]{1,0:T(8,128)S(1)} %convolution_multiply_fusion.4), channel_id=3, replica_groups=mesh['cell'=8,'gene'=4] {'gene'}, dimensions={0}, use_global_device_ids=true | all-gather | bytes 327680 | tf_op jit(solution)/shard_map/all_gather | solution.py:10
  96.8 0.7 multiply_add_fusion
  97.5 0.9 copy.17
  98.4 0.8 add_convert_fusion
  99.2 30.4 %reduce-scatter.9.cloned.1.call-done = f32[80,64]{1,0:T(8,128)} async-done(((f32[640,64]{1,0:T(8,128)}), f32[80,64]{1,0:T(8,128)}) %reduce-scatter.9.cloned.1.call-update) | async-done | bytes 20496
  129.7 0.8 copy.18
  130.5 1.0 add_bitcast_fusion
  131.5 9.3 %all-gather.3 = f32[8,80,64]{1,2,0:T(8,128)S(1)} all-gather(f32[1,80,64]{1,2,0:T(8,128)S(1)} %add_bitcast_fusion), channel_id=1, replica_groups=mesh['cell'=8,'gene'=4] {'cell'}, dimensions={0}, use_global_device_ids=true | all-gather | bytes 184320 | tf_op jit(solution)/shard_map/all_gather | solution.py:63
  140.9 0.8 reshape.23
  (31 shorter events, 1.6 us)
Async XLA Ops:
  7.2 1.2 copy-start.2
  7.2 2.9 %copy-start = (s32[256,640]{1,0:T(8,128)S(1)}, s32[256,640]{1,0:T(8,128)}, u32[]{:S(2)}) copy-start(s32[256,640]{1,0:T(8,128)} %param.6) | copy-start | bytes 1966084
  7.2 50.2 %reduce-scatter.7.cloned.1.call-start = ((), (), s32[]{:S(2)}) async-start(), calls=%async_computation.2 | async-start | bytes 368640
  10.0 13.6 %copy-start.3 = (f32[64,256]{1,0:T(8,128)S(1)}, f32[64,256]{1,0:T(8,128)}, u32[]{:S(2)}) copy-start(f32[64,256]{1,0:T(8,128)} %param.7) | copy-start | bytes 196612
  25.2 0.9 copy-start.6
  25.2 104.4 %reduce-scatter.9.cloned.1.call-start = ((), (), s32[]{:S(2)}) async-start(), calls=%async_computation.3 | async-start | bytes 368640
  40.0 0.8 copy-start.5
  41.0 55.8 %copy-start.4 = (f32[64,256]{1,0:T(8,128)}, f32[64,256]{1,0:T(8,128)S(1)}, u32[]{:S(2)}) copy-start(f32[64,256]{1,0:T(8,128)S(1)} %multiply_add_fusion.1) | copy-start | bytes 196612
  68.8 12.7 %copy-start.1 = (f32[640,64]{0,1:T(8,128)}, f32[640,64]{0,1:T(8,128)S(1)}, u32[]{:S(2)}) copy-start(f32[640,64]{0,1:T(8,128)S(1)} %reshape.21) | copy-start | bytes 491524
Sparse Core Ops, SparseCore 0:
  25.4 32.0 reduce-scatter.6
  98.5 31.0 reduce-scatter.8
